TPU v7x, 256 devices: a whole 4x4x8 slice. The times are simulated.
256 devices in a mesh: row: 8 (over y, x_lo), col: 32 (over z, x_hi, core).
Axes of the slice: x: 4 (x_hi: 2, x_lo: 2; x = x_hi * 2 + x_lo), y: 4, z: 8, core: 2. Of those that a mesh axis runs over, the one named last changes fastest.
Arguments:
- grad_out: bfloat16 [3072, 8192], P('row', 'col'), may hold values from -6 to 6
- gate_act: bfloat16 [3072, 28672], P('row', 'col'), may hold values from -6 to 6
- up_act: bfloat16 [3072, 28672], P('row', 'col'), may hold values from -6 to 6
- down_weight: bfloat16 [28672, 8192], P('col', 'row'), may hold values from -0.0625 to 0.0625
Outputs:
- grad_gate: bfloat16 [3072, 28672], P('row', 'col')
- grad_up: bfloat16 [3072, 28672], P('row', 'col')
- grad_weight: float32 [28672, 8192], P('col', 'row')
All inputs are finite; a program needn't handle non-finite values.
Results may differ from a plain program's by a relative error of at most 0.0028.
Values may be sent and summed in bfloat16 or wider, within the bound.
A program may use at most 128 MiB of HBM per device.

v0:
```python
import jax
import jax.numpy as jnp
from jax import lax
from jax.sharding import PartitionSpec as P


def collect_features(grad_out):
    return lax.all_gather(grad_out, "col", axis=1, tiled=True)


def on_device(grad_out, gate_act, up_act, down_weight):
    token_major = lax.all_to_all(
        collect_features(grad_out), "row", split_axis=1, concat_axis=0, tiled=True
    )
    grad_rows = collect_features(grad_out)
    grad_hidden = lax.dot_general(
        grad_rows,
        lax.all_gather(down_weight, "row", axis=1, tiled=True),
        (((1,), (1,)), ((), ())),
        preferred_element_type=jnp.float32,
    )
    gate_value = gate_act.astype(jnp.float32)
    up_value = up_act.astype(jnp.float32)
    sigmoid_gate = jax.nn.sigmoid(gate_value)
    swish = gate_value * sigmoid_gate
    grad_gate = (
        grad_hidden * up_value * sigmoid_gate * (1.0 + gate_value * (1.0 - sigmoid_gate))
    ).astype(jnp.bfloat16)
    grad_up = (grad_hidden * swish).astype(jnp.bfloat16)
    hidden = (swish * up_value).astype(jnp.bfloat16)
    grad_weight = lax.dot_general(
        lax.all_gather(hidden, "row", axis=0, tiled=True),
        token_major,
        (((0,), (0,)), ((), ())),
        preferred_element_type=jnp.float32,
    )
    return (grad_gate, grad_up, grad_weight)


def solution(mesh):
    placed = (P("row", "col"), P("row", "col"), P("row", "col"), P("col", "row"))
    return jax.shard_map(
        on_device,
        mesh=mesh,
        in_specs=placed,
        out_specs=(P("row", "col"), P("row", "col"), P("col", "row")),
        check_vma=False,
    )
```

profile of v0, /device:TPU:1, one launch (start us, length us, event | category | flops | bytes accessed | tf_op | source)
XLA Modules:
  0.0 607.0 jit_solution(11016101793268797252)
XLA Ops:
  7.2 0.0 all-gather.4.cloned.1.call-start
  7.2 1.7 copy.7
  9.0 0.0 all-gather.4.cloned.1.call-update
  9.0 0.0 all-gather.6.cloned.1.call-start
  9.0 0.7 all-gather.6.cloned.1.call-update
  9.7 0.0 all-gather.8.cloned.1.call-start
  9.8 99.5 %all-gather.4.cloned.1.call-done = bf16[384,8192]{0,1:T(8,128)(2,1)} async-done(((bf16[384,256]{0,1:T(8,128)(2,1)}), bf16[384,8192]{0,1:T(8,128)(2,1)}) %all-gather.4.cloned.1.call-update) | async-done | bytes 6291472 | tf_op jit(solution)/shard_map/all_gather | solution.py:8
  109.2 286.9 %all-gather.6.cloned.1.call-done = bf16[896,8192]{1,0:T(8,128)(2,1)} async-done(((bf16[896,1024]{1,0:T(8,128)(2,1)}), bf16[896,8192]{1,0:T(8,128)(2,1)}) %all-gather.6.cloned.1.call-update) | async-done | bytes 14680080 | tf_op jit(solution)/shard_map/all_gather | solution.py:18
  396.1 13.8 %multiply_convert_fusion = (bf16[384,896]{1,0:T(8,128)(2,1)}, bf16[384,896]{1,0:T(8,128)(2,1)}, bf16[384,896]{1,0:T(8,128)(2,1)}) fusion(bf16[384,896]{1,0:T(8,128)(2,1)} %param.5, bf16[384,896]{1,0:T(8,128)(2,1)} %param.6, bf16[384,8192]{0,1:T(8,128)(2,1)} %all-gather.4.cloned.1.call-done, bf16[896,8192]{1,0:T(8,128)(2,1)} %all-gather.6.cloned.1.call-done), kind=kOutput, calls=%fused_computation.13 | convolution fusion | flops 5642993664 | bytes 24412160 | tf_op jit(solution)/shard_map/dot_general | solution.py:16
  409.9 0.0 all-gather.8.cloned.1.call-update
  409.9 136.3 %all_to_all.19 = bf16[384,8,1024]{0,2,1:T(8,128)(2,1)} all-to-all(bf16[384,8,1024]{0,2,1:T(8,128)(2,1)} %bitcast.8), channel_id=1, replica_groups=mesh['row'=8,'col'=32] {'row'}, dimensions={1} | all-to-all | bytes 12582912 | tf_op jit(solution)/shard_map/all_to_all | solution.py:12
  546.2 8.6 %copy.8 = bf16[8,384,1024]{2,1,0:T(8,128)(2,1)} copy(bf16[8,384,1024]{1,2,0:T(8,128)(2,1)} %bitcast.7) | data formatting | bytes 12582912 | tf_op jit(solution)/shard_map/all_to_all | solution.py:12
  554.9 34.7 %all-gather.8.cloned.1.call-done = bf16[3072,896]{1,0:T(8,128)(2,1)} async-done(((bf16[384,896]{1,0:T(8,128)(2,1)}), bf16[3072,896]{1,0:T(8,128)(2,1)}) %all-gather.8.cloned.1.call-update) | async-done | bytes 5505040 | tf_op jit(solution)/shard_map/all_gather | solution.py:32
  589.6 10.8 %fusion.8 = f32[896,1024]{1,0:T(8,128)} fusion(bf16[3072,896]{1,0:T(8,128)(2,1)} %all-gather.8.cloned.1.call-done, bf16[3072,1024]{1,0:T(8,128)(2,1)} %bitcast.9), kind=kOutput, calls=%fused_computation.14 | convolution fusion | flops 5637144576 | bytes 15466496 | tf_op jit(solution)/shard_map/dot_general | solution.py:31
Async XLA Ops:
  7.2 102.1 %all-gather.4.cloned.1.call-start = ((), (), s32[]{:S(2)}) async-start(), calls=%async_computation.1 | async-start | bytes 6488064 | tf_op jit(solution)/shard_map/all_gather | solution.py:8
  9.0 387.1 %all-gather.6.cloned.1.call-start = ((), (), s32[]{:S(2)}) async-start(), calls=%async_computation.2 | async-start | bytes 16515072 | tf_op jit(solution)/shard_map/all_gather | solution.py:18
  9.7 579.9 %all-gather.8.cloned.1.call-start = ((), (), s32[]{:S(2)}) async-start(), calls=%async_computation.3 | async-start | bytes 6193152 | tf_op jit(solution)/shard_map/all_gather | solution.py:32
Sparse Core Ops, SparseCore 0:
  11.3 97.8 all-gather.3
  111.0 285.0 all-gather.5
  410.1 179.5 all-gather.7
where the time goes:
time: 607 us
  waiting for transfers between devices  422 us (70%)
  blocking collectives  136 us (22%)
  matrix products  24.7 us (4%)
  between operations  13.7 us (2%)
  local copies, waits for them, and re-layouts  10.4 us (2%)
    all_gather x1, waiting for transfers between devices, on_device(): lax.all_gather(down_weight, 'row', axis=1, tiled=True)  287 us
    all_to_all x1, blocking collectives, on_device(): lax.all_to_all(collect_features(grad_out), 'row', split_axis=1, concat_ax...  136 us
    all_gather x1, waiting for transfers between devices, collect_features(): return lax.all_gather(grad_out, 'col', axis=1, tiled=True)  99.5 us
    all_gather x1, waiting for transfers between devices, on_device(): lax.all_gather(hidden, 'row', axis=0, tiled=True)  34.7 us
    dot_general x1, matrix products, on_device(): lax.dot_general(grad_rows, lax.all_gather(down_weight, 'row', axis=1, til...  13.8 us
  transfers between devices with their start and end apart: 3, of which 3 were waited for; matrix products, arithmetic and copies ran while one was open for 1% of the time, Pallas kernels for 0%

commit v1 on v0

--- a/solution.py
+++ b/solution.py
@@ -5,7 +5,9 @@
 
 
 def collect_features(grad_out):
-    return lax.all_gather(grad_out, "col", axis=1, tiled=True)
+    return jnp.concatenate(
+        lax.all_to_all(jnp.stack([grad_out] * lax.axis_size("col")), "col", 0, 0), axis=1
+    )
 
 
 def on_device(grad_out, gate_act, up_act, down_weight):

time: 607 us -> 579 us (0.954)
  waiting for transfers between devices: 422 us -> 240 us
  blocking collectives: 136 us -> 290 us
    all_to_all x0 -> x1, blocking collectives: none -> 153 us  [collect_features(): lax.all_to_all(jnp.stack([grad_out] * lax.axis_size('col')), 'col', 0, 0)]
    all_gather x1 -> x0, waiting for transfers between devices: 99.5 us -> none  [collect_features(): return lax.all_gather(grad_out, 'col', axis=1, tiled=True)]
    all_gather x1, waiting for transfers between devices: 287 us -> 204 us  [on_device(): lax.all_gather(down_weight, 'row', axis=1, tiled=True)]
  transfers between devices with their start and end apart: 3 -> 2, of which waited for: 3 -> 2; matrix products, arithmetic and copies ran while one was open for 1% -> 2% of each run, Pallas kernels for 0% -> 0%
where the time goes in v1:
time: 579 us
  blocking collectives  290 us (50%)
  waiting for transfers between devices  240 us (41%)
  matrix products  24.5 us (4%)
  between operations  14.1 us (2%)
  local copies, waits for them, and re-layouts  10.7 us (2%)
    all_gather x1, waiting for transfers between devices, on_device(): lax.all_gather(down_weight, 'row', axis=1, tiled=True)  204 us
    all_to_all x1, blocking collectives, collect_features(): lax.all_to_all(jnp.stack([grad_out] * lax.axis_size('col')), 'col', 0, 0)  153 us
    all_to_all x1, blocking collectives, on_device(): lax.all_to_all(collect_features(grad_out), 'row', split_axis=1, concat_ax...  137 us
    all_gather x1, waiting for transfers between devices, on_device(): lax.all_gather(hidden, 'row', axis=0, tiled=True)  34.9 us
    dot_general x1, matrix products, on_device(): lax.dot_general(grad_rows, lax.all_gather(down_weight, 'row', axis=1, til...  13.6 us
  transfers between devices with their start and end apart: 2, of which 2 were waited for; matrix products, arithmetic and copies ran while one was open for 2% of the time, Pallas kernels for 0%

profile of v1, /device:TPU:1, one launch (start us, length us, event | category | flops | bytes accessed | tf_op | source)
XLA Modules:
  0.0 578.8 jit_solution(2369960090843476481)
XLA Ops:
  7.2 0.0 all-gather.3.cloned.1.call-start
  7.2 0.7 all-gather.3.cloned.1.call-update
  7.9 0.0 all-gather.5.cloned.1.call-start
  7.9 1.1 copy.7
  9.0 0.9 stack.2
  10.0 0.0 copy-start
  10.0 0.0 copy-start.1
  10.0 153.0 %all_to_all.25 = bf16[32,384,256]{1,2,0:T(8,128)(2,1)} all-to-all(bf16[32,384,256]{1,2,0:T(8,128)(2,1)S(1)} %stack.2), channel_id=1, replica_groups=mesh['row'=8,'col'=32] {'col'}, dimensions={0} | all-to-all | bytes 12582912 | tf_op jit(solution)/shard_map/all_to_all | solution.py:9
  163.0 204.3 %all-gather.3.cloned.1.call-done = bf16[896,8192]{1,0:T(8,128)(2,1)} async-done(((bf16[896,1024]{1,0:T(8,128)(2,1)}), bf16[896,8192]{1,0:T(8,128)(2,1)}) %all-gather.3.cloned.1.call-update) | async-done | bytes 14680080 | tf_op jit(solution)/shard_map/all_gather | solution.py:20
  367.3 0.0 copy-done
  367.3 0.0 copy-done.1
  367.3 13.6 %multiply_convert_fusion = (bf16[384,896]{1,0:T(8,128)(2,1)}, bf16[384,896]{1,0:T(8,128)(2,1)}, bf16[384,896]{1,0:T(8,128)(2,1)}) fusion(bf16[384,896]{1,0:T(8,128)(2,1)S(1)} %copy-done, bf16[384,896]{1,0:T(8,128)(2,1)S(1)} %copy-done.1, bf16[384,8192]{0,1:T(8,128)(2,1)} %bitcast.11, bf16[896,8192]{1,0:T(8,128)(2,1)} %all-gather.3.cloned.1.call-done), kind=kOutput, calls=%fused_computation.13 | convolution fusion | flops 5642993664 | bytes 24412160 | tf_op jit(solution)/shard_map/dot_general | solution.py:18
  380.9 0.0 all-gather.5.cloned.1.call-update
  381.0 136.7 %all_to_all.26 = bf16[384,8,1024]{0,2,1:T(8,128)(2,1)} all-to-all(bf16[384,8,1024]{0,2,1:T(8,128)(2,1)} %bitcast.12), channel_id=1, replica_groups=mesh['row'=8,'col'=32] {'row'}, dimensions={1} | all-to-all | bytes 12582912 | tf_op jit(solution)/shard_map/all_to_all | solution.py:14
  517.6 8.6 %copy.8 = bf16[8,384,1024]{2,1,0:T(8,128)(2,1)} copy(bf16[8,384,1024]{1,2,0:T(8,128)(2,1)} %bitcast.13) | data formatting | bytes 12582912 | tf_op jit(solution)/shard_map/all_to_all | solution.py:14
  526.2 34.9 %all-gather.5.cloned.1.call-done = bf16[3072,896]{1,0:T(8,128)(2,1)} async-done(((bf16[384,896]{1,0:T(8,128)(2,1)}), bf16[3072,896]{1,0:T(8,128)(2,1)}) %all-gather.5.cloned.1.call-update) | async-done | bytes 5505040 | tf_op jit(solution)/shard_map/all_gather | solution.py:34
  561.1 10.8 %fusion.8 = f32[896,1024]{1,0:T(8,128)} fusion(bf16[3072,896]{1,0:T(8,128)(2,1)} %all-gather.5.cloned.1.call-done, bf16[3072,1024]{1,0:T(8,128)(2,1)} %bitcast.14), kind=kOutput, calls=%fused_computation.14 | convolution fusion | flops 5637144576 | bytes 15466496 | tf_op jit(solution)/shard_map/dot_general | solution.py:33
Async XLA Ops:
  7.2 360.1 %all-gather.3.cloned.1.call-start = ((), (), s32[]{:S(2)}) async-start(), calls=%async_computation.2 | async-start | bytes 16515072 | tf_op jit(solution)/shard_map/all_gather | solution.py:20
  7.9 553.2 %all-gather.5.cloned.1.call-start = ((), (), s32[]{:S(2)}) async-start(), calls=%async_computation.3 | async-start | bytes 6193152 | tf_op jit(solution)/shard_map/all_gather | solution.py:34
  10.0 357.3 %copy-start = (bf16[384,896]{1,0:T(8,128)(2,1)S(1)}, bf16[384,896]{1,0:T(8,128)(2,1)}, u32[]{:S(2)}) copy-start(bf16[384,896]{1,0:T(8,128)(2,1)} %param.5) | copy-start | bytes 2064388
  10.0 357.3 %copy-start.1 = (bf16[384,896]{1,0:T(8,128)(2,1)S(1)}, bf16[384,896]{1,0:T(8,128)(2,1)}, u32[]{:S(2)}) copy-start(bf16[384,896]{1,0:T(8,128)(2,1)} %param.6) | copy-start | bytes 2064388
Sparse Core Ops, SparseCore 0:
  9.8 357.4 all-gather.2
  381.1 179.9 all-gather.4
